TPU v7x, 512 devices: a whole 4x4x16 slice. The times are simulated.
512 devices in a mesh: row: 8 (over z_hi, core), col: 16 (over y, z_lo), depth: 4 (over x).
Axes of the slice: x: 4, y: 4, z: 16 (z_hi: 4, z_lo: 4; z = z_hi * 4 + z_lo), core: 2. Of those that a mesh axis runs over, the one named last changes fastest.
Arguments:
- values: bfloat16 [768, 16, 128, 128], P(('row', 'col')), may hold values from -0.47851562 to 0.47851562
- columns: int32 [768, 16], replicated, may hold values from 0 to 767, as said below
Outputs:
- purified: bfloat16 [768, 16, 128, 128], P(('row', 'col'), 'depth')
Inputs may be any that keep to these rules, and one draw needn't show every extreme that they name: Each block row a names 16 different block columns, a itself among them, all within 8 of a around the cycle of 768 block rows (indices wrap).
All inputs are finite; a program needn't handle non-finite values.
Results may differ from a plain program's by a relative error of at most 0.0047.
Values may be sent and summed in bfloat16 or wider, within the bound.
A program may use at most 128 MiB of HBM per device.

v0:
```python
import jax
import jax.numpy as jnp
from jax import lax
from jax.sharding import PartitionSpec as P

HB = 8


def passed_along(value, axis, by):
    peers = lax.axis_size(axis)
    return lax.ppermute(value, axis, [(i, (i + by) % peers) for i in range(peers)])


def matched_blocks(nearby, band_start, own_cols, target_cols, columns):
    total_blocks = columns.shape[0]
    band_count = nearby.shape[0]
    slot_count = nearby.shape[1]
    partner_cols = jnp.take(columns, own_cols, axis=0)
    same_column = partner_cols[:, :, None, :] == target_cols[:, None, :, None]
    slot_ids = jnp.arange(slot_count, dtype=jnp.int32)
    present = jnp.any(same_column, axis=3)
    chosen = jnp.sum(jnp.where(same_column, slot_ids, 0), axis=3)
    offset = jnp.mod(own_cols - band_start, total_blocks)
    inside = offset < band_count
    usable = inside[:, :, None] & present
    flat_index = jnp.where(
        usable, offset[:, :, None] * slot_count + chosen, band_count * slot_count
    )
    flat_blocks = nearby.reshape(band_count * slot_count, nearby.shape[2], nearby.shape[3])
    return jnp.take(flat_blocks, flat_index, axis=0, mode="fill", fill_value=0)


def local(values, columns):
    own_rows, slot_count, block_size, _ = values.shape
    layers = lax.axis_size("depth")
    quarter = slot_count // layers
    layer_index = lax.axis_index("depth")
    group_index = lax.axis_index(("row", "col"))
    first_row = group_index * own_rows
    own_cols = lax.dynamic_slice_in_dim(columns, first_row, own_rows, 0)
    target_cols = lax.dynamic_slice_in_dim(own_cols, layer_index * quarter, quarter, 1)
    hop_count = (HB + own_rows - 1) // own_rows
    reach_last = HB - (hop_count - 1) * own_rows
    lower_parts = []
    upper_parts = []
    for hop_step in range(1, hop_count + 1):
        edge_rows = own_rows if hop_step < hop_count else reach_last
        from_lower = passed_along(values[own_rows - edge_rows :], ("row", "col"), hop_step)
        from_upper = passed_along(values[:edge_rows], ("row", "col"), -hop_step)
        lower_parts.insert(0, from_lower)
        upper_parts.append(from_upper)
    below_rows = jnp.concatenate(lower_parts, axis=0)
    above_rows = jnp.concatenate(upper_parts, axis=0)
    nearby = jnp.concatenate([below_rows, values, above_rows], axis=0)
    selected = matched_blocks(nearby, first_row - HB, own_cols, target_cols, columns)
    square32 = jnp.einsum("aixy,aijyz->ajxz", values, selected, preferred_element_type=jnp.float32)
    square = square32.astype(jnp.bfloat16)
    whole_square = lax.all_gather(square, "depth", axis=1, tiled=True)
    cube32 = jnp.einsum(
        "aixy,aijyz->ajxz", whole_square, selected, preferred_element_type=jnp.float32
    )
    return (3.0 * square32 - 2.0 * cube32).astype(jnp.bfloat16)


def solution(mesh):
    placed = (P(("row", "col"), None, None, None), P())
    return jax.shard_map(
        local,
        mesh=mesh,
        in_specs=placed,
        out_specs=P(("row", "col"), "depth", None, None),
        check_vma=False,
    )
```

profile of v0, /device:TPU:1, one launch (start us, length us, event | category | flops | bytes accessed | tf_op | source)
XLA Modules:
  0.0 335.9 jit_solution(13076159911926167194)
XLA Ops:
  6.5 0.0 copy-start
  6.5 0.0 all-gather.2.cloned.1.call-start
  6.5 4.6 %collective-permute-start.1 = (bf16[6,16,128,128]{3,2,1,0:T(8,128)(2,1)}, bf16[6,16,128,128]{3,2,1,0:T(8,128)(2,1)}, u32[]{:S(2)}, u32[]{:S(2)}) collective-permute-start(bf16[6,16,128,128]{3,2,1,0:T(8,128)(2,1)} %param.2), channel_id=1, source_target_pairs={{0,4},{4,8},{8,12},{12,16},{16,20},{20,24},{24,28},{28,32},{32,36}... | collective-permute-start | bytes 9437192 | tf_op jit(solution)/shard_map/ppermute | solution.py:11
  11.2 7.6 %collective-permute-start.2 = (bf16[6,16,128,128]{3,2,1,0:T(8,128)(2,1)}, bf16[6,16,128,128]{3,2,1,0:T(8,128)(2,1)}, u32[]{:S(2)}, u32[]{:S(2)}) collective-permute-start(bf16[6,16,128,128]{3,2,1,0:T(8,128)(2,1)} %param.2), channel_id=1, source_target_pairs={{0,508},{4,0},{8,4},{12,8},{16,12},{20,16},{24,20},{28,24},{32,28}... | collective-permute-start | bytes 9437192 | tf_op jit(solution)/shard_map/ppermute | solution.py:11
  18.8 3.2 fusion.18
  22.0 1.9 collective-permute-start
  23.9 6.7 %collective-permute-start.3 = (bf16[2,16,128,128]{3,2,1,0:T(8,128)(2,1)}, bf16[2,16,128,128]{3,2,1,0:T(8,128)(2,1)}, u32[]{:S(2)}, u32[]{:S(2)}) collective-permute-start(bf16[2,16,128,128]{3,2,1,0:T(8,128)(2,1)} %get-tuple-element.7), channel_id=1, source_target_pairs={{0,504},{4,508},{8,0},{12,4},{16,8},{20,12},{24,16},{28,20},{32,24... | collective-permute-start | bytes 3145736 | tf_op jit(solution)/shard_map/ppermute | solution.py:11
  30.6 1.0 copy.39
  31.5 0.5 compare_and_fusion.1
  32.1 0.6 reshape.50
  32.7 0.7 pad_clamp_fusion.1
  33.3 1.4 dynamic_slice.7
  34.7 0.8 copy.41
  35.5 1.2 gather_fusion
  36.7 0.9 broadcast_select_fusion.7
  37.6 0.6 compare_reduce_fusion
  38.1 0.6 fusion.14
  38.7 0.1 copy.43
  38.9 0.1 reshape.58
  39.0 0.1 copy.42
  39.1 138.4 %collective-permute-done = bf16[2,16,128,128]{3,2,1,0:T(8,128)(2,1)} collective-permute-done((bf16[2,16,128,128]{3,2,1,0:T(8,128)(2,1)}, bf16[2,16,128,128]{3,2,1,0:T(8,128)(2,1)}, u32[]{:S(2)}, u32[]{:S(2)}) %collective-permute-start) | collective-permute-done | bytes 1048608 | tf_op jit(solution)/shard_map/ppermute | solution.py:11
  177.5 2.4 constant_dynamic-update-slice_fusion.4
  179.8 0.0 collective-permute-done.1
  179.8 3.9 %constant_dynamic-update-slice_fusion.3 = bf16[22,16,128,128]{3,2,1,0:T(8,128)(2,1)} fusion(bf16[22,16,128,128]{3,2,1,0:T(8,128)(2,1)} %constant_dynamic-update-slice_fusion.4, bf16[6,16,128,128]{3,2,1,0:T(8,128)(2,1)} %collective-permute-done.1), kind=kLoop, calls=%fused_computation.30 | loop fusion | bytes 6291456
  183.8 0.0 copy-done
  183.8 2.1 constant_dynamic-update-slice_fusion.2
  185.9 0.0 collective-permute-done.2
  185.9 4.0 %constant_dynamic-update-slice_fusion.1 = bf16[22,16,128,128]{3,2,1,0:T(8,128)(2,1)} fusion(bf16[22,16,128,128]{3,2,1,0:T(8,128)(2,1)} %constant_dynamic-update-slice_fusion.2, bf16[6,16,128,128]{3,2,1,0:T(8,128)(2,1)} %collective-permute-done.2), kind=kLoop, calls=%fused_computation.28 | loop fusion | bytes 6291456
  189.8 50.2 %collective-permute-done.3 = bf16[2,16,128,128]{3,2,1,0:T(8,128)(2,1)} collective-permute-done((bf16[2,16,128,128]{3,2,1,0:T(8,128)(2,1)}, bf16[2,16,128,128]{3,2,1,0:T(8,128)(2,1)}, u32[]{:S(2)}, u32[]{:S(2)}) %collective-permute-start.3) | collective-permute-done | bytes 1048608 | tf_op jit(solution)/shard_map/ppermute | solution.py:11
  240.1 2.3 constant_dynamic-update-slice_fusion
  242.4 15.5 %gather_fusion.1 = bf16[384,128,128]{2,1,0:T(8,128)(2,1)} fusion(bf16[352,128,128]{2,1,0:T(8,128)(2,1)} %bitcast.1, s32[1024]{0:T(1024)S(1)} %pad_clamp_fusion), kind=kCustom, calls=%fused_computation.1 | custom fusion | bytes 25167360 | tf_op jit(solution)/shard_map/jit(_take)/gather | solution.py:30
  257.9 7.9 %fusion = f32[6,4,128,128,1]{3,2,1,4,0:T(8,128)S(1)} fusion(bf16[6,16,4,128,128]{4,3,2,1,0:T(8,128)(2,1)} %bitcast.62, pred[6,16,4]{2,1,0:T(8,128)(4,1)S(1)} %copy.42, bf16[6,16,128,128]{3,2,1,0:T(8,128)(2,1)S(1)} %copy-done), kind=kOutput, calls=%fused_computation.3 | convolution fusion | flops 1616904192 | bytes 17301888 | tf_op jit(solution)/shard_map/aixy,aijyz->ajxz/dot_general | solution.py:56
  265.8 0.0 copy-start.1
  265.8 1.1 copy-done.1
  266.9 1.0 fusion.13
  268.0 0.0 all-gather.2.cloned.1.call-update
  268.0 51.1 %all-gather.2.cloned.1.call-done = bf16[6,16,128,128]{2,3,1,0:T(8,128)(2,1)} async-done(((bf16[6,4,128,128]{2,3,1,0:T(8,128)(2,1)}), bf16[6,16,128,128]{2,3,1,0:T(8,128)(2,1)}) %all-gather.2.cloned.1.call-update) | async-done | bytes 3145744 | tf_op jit(solution)/shard_map/all_gather | solution.py:58
  319.1 8.7 %fusion.10 = bf16[6,4,128,128]{2,3,1,0:T(8,128)(2,1)S(1)} fusion(bf16[6,16,128,128]{2,3,1,0:T(8,128)(2,1)} %all-gather.2.cloned.1.call-done, bf16[6,16,4,128,128]{4,3,2,1,0:T(8,128)(2,1)} %bitcast.63, pred[6,16,4]{2,1,0:T(8,128)(4,1)S(1)} %copy.42, f32[6,4,128,128,1]{3,2,1,4,0:T(8,128)} %copy-done.1), kind=kOutput, calls=%fused_computation.14 | convolution fusion | flops 1618477056 | bytes 18088320 | tf_op jit(solution)/shard_map/aixy,aijyz->ajxz/dot_general | solution.py:59
  327.9 1.2 copy.47
  (4 shorter events, 0.1 us)
Async XLA Ops:
  6.5 177.3 %copy-start = (bf16[6,16,128,128]{3,2,1,0:T(8,128)(2,1)S(1)}, bf16[6,16,128,128]{3,2,1,0:T(8,128)(2,1)}, u32[]{:S(2)}) copy-start(bf16[6,16,128,128]{3,2,1,0:T(8,128)(2,1)} %param.2) | copy-start | bytes 9437188
  6.5 312.6 %all-gather.2.cloned.1.call-start = ((), (), s32[]{:S(2)}) async-start(), calls=%async_computation | async-start | bytes 3932160 | tf_op jit(solution)/shard_map/all_gather | solution.py:58
  6.5 173.3 %collective-permute-start.1 = (bf16[6,16,128,128]{3,2,1,0:T(8,128)(2,1)}, bf16[6,16,128,128]{3,2,1,0:T(8,128)(2,1)}, u32[]{:S(2)}, u32[]{:S(2)}) collective-permute-start(bf16[6,16,128,128]{3,2,1,0:T(8,128)(2,1)} %param.2), channel_id=1, source_target_pairs={{0,4},{4,8},{8,12},{12,16},{16,20},{20,24},{24,28},{28,32},{32,36}... | collective-permute-start | bytes 9437192 | tf_op jit(solution)/shard_map/ppermute | solution.py:11
  11.2 174.7 %collective-permute-start.2 = (bf16[6,16,128,128]{3,2,1,0:T(8,128)(2,1)}, bf16[6,16,128,128]{3,2,1,0:T(8,128)(2,1)}, u32[]{:S(2)}, u32[]{:S(2)}) collective-permute-start(bf16[6,16,128,128]{3,2,1,0:T(8,128)(2,1)} %param.2), channel_id=1, source_target_pairs={{0,508},{4,0},{8,4},{12,8},{16,12},{20,16},{24,20},{28,24},{32,28}... | collective-permute-start | bytes 9437192 | tf_op jit(solution)/shard_map/ppermute | solution.py:11
  22.0 155.5 %collective-permute-start = (bf16[2,16,128,128]{3,2,1,0:T(8,128)(2,1)}, bf16[2,16,128,128]{3,2,1,0:T(8,128)(2,1)}, u32[]{:S(2)}, u32[]{:S(2)}) collective-permute-start(bf16[2,16,128,128]{3,2,1,0:T(8,128)(2,1)} %get-tuple-element.8), channel_id=1, source_target_pairs={{0,8},{4,12},{8,16},{12,20},{16,24},{20,28},{24,32},{28,36},{32,40... | collective-permute-start | bytes 3145736 | tf_op jit(solution)/shard_map/ppermute | solution.py:11
  23.9 216.2 %collective-permute-start.3 = (bf16[2,16,128,128]{3,2,1,0:T(8,128)(2,1)}, bf16[2,16,128,128]{3,2,1,0:T(8,128)(2,1)}, u32[]{:S(2)}, u32[]{:S(2)}) collective-permute-start(bf16[2,16,128,128]{3,2,1,0:T(8,128)(2,1)} %get-tuple-element.7), channel_id=1, source_target_pairs={{0,504},{4,508},{8,0},{12,4},{16,8},{20,12},{24,16},{28,20},{32,24... | collective-permute-start | bytes 3145736 | tf_op jit(solution)/shard_map/ppermute | solution.py:11
  265.8 1.1 copy-start.1
Sparse Core Ops, SparseCore 0:
  268.1 50.9 all-gather.1
where the time goes:
time: 336 us
  waiting for transfers between devices  240 us (71%)
  local copies, waits for them, and re-layouts  40.9 us (12%)
  starting transfers between devices  20.8 us (6%)
  matrix products  16.6 us (5%)
  between operations  13.5 us (4%)
  other arithmetic  4.28 us (1%)
    ppermute x4, waiting for transfers between devices, passed_along(): lax.ppermute(value, axis, [(i, (i + by) % peers) for i in range(peers)])  189 us
    all_gather x1, waiting for transfers between devices, local(): whole_square = lax.all_gather(square, 'depth', axis=1, tiled=True)  51.1 us
    ppermute x4, starting transfers between devices, passed_along(): lax.ppermute(value, axis, [(i, (i + by) % peers) for i in range(peers)])  20.8 us
    gather x1, local copies, waits for them, and re-layouts, matched_blocks(): return jnp.take(flat_blocks, flat_index, axis=0, mode='fill', fill_value=0)  15.5 us
    unnamed x9, local copies, waits for them, and re-layouts  14.4 us
    dot_general x1, matrix products, local(): jnp.einsum('aixy,aijyz->ajxz', whole_square, selected, preferred_element_...  8.72 us
    dot_general x1, matrix products, local(): jnp.einsum('aixy,aijyz->ajxz', values, selected, preferred_element_type=j...  7.87 us
  transfers between devices with their start and end apart: 5, of which 3 were waited for; matrix products, arithmetic and copies ran while one was open for 7% of the time, Pallas kernels for 0%

commit v1 on v0

--- a/solution.py
+++ b/solution.py
@@ -4,6 +4,26 @@
 from jax.sharding import PartitionSpec as P
 
 HB = 8
+
+
+def drive_steps_all(w_in, mesh_name, in_array):
+    newest = lax.axis_size(mesh_name)
+    step_out = lax.axis_index(mesh_name)
+    n_now, y2, tmp = (newest, step_out, w_in.shape[1])
+    queue = [(ix, (ix + 1) % n_now) for ix in range(n_now)]
+    latest = n_now // 2
+    cards = [(ix, (ix - 1) % n_now) for ix in range(n_now)]
+    built = in_array(w_in, y2 * tmp)
+    side_arr = met_up = w_in
+    for rr in range(1, latest + 1):
+        side_arr = lax.ppermute(side_arr, mesh_name, queue)
+        if rr < n_now - latest:
+            met_up = lax.ppermute(met_up, mesh_name, cards)
+            plain = in_array(met_up, (y2 + rr) % n_now * tmp)
+            built = built + plain
+        mid_arr = in_array(side_arr, (y2 - rr) % n_now * tmp)
+        built = built + mid_arr
+    return built
 
 
 def passed_along(value, axis, by):
@@ -55,9 +75,15 @@
     selected = matched_blocks(nearby, first_row - HB, own_cols, target_cols, columns)
     square32 = jnp.einsum("aixy,aijyz->ajxz", values, selected, preferred_element_type=jnp.float32)
     square = square32.astype(jnp.bfloat16)
-    whole_square = lax.all_gather(square, "depth", axis=1, tiled=True)
-    cube32 = jnp.einsum(
-        "aixy,aijyz->ajxz", whole_square, selected, preferred_element_type=jnp.float32
+    cube32 = drive_steps_all(
+        square,
+        "depth",
+        lambda shard, offset_2: jnp.einsum(
+            "aixy,aijyz->ajxz",
+            shard,
+            lax.dynamic_slice_in_dim(selected, offset_2, shard.shape[1], axis=1),
+            preferred_element_type=jnp.float32,
+        ),
     )
     return (3.0 * square32 - 2.0 * cube32).astype(jnp.bfloat16)
 

time: 336 us -> 329 us (0.979)
  waiting for transfers between devices: 240 us -> 216 us
  local copies, waits for them, and re-layouts: 40.9 us -> 54.5 us
  between operations: 13.5 us -> 0.26 us
  starting transfers between devices: 20.8 us -> 29 us
  other arithmetic: 4.28 us -> 9.78 us
    all_gather x1 -> x0, waiting for transfers between devices: 51.1 us -> none  [local(): whole_square = lax.all_gather(square, 'depth', axis=1, tiled=True)]
    ppermute x0 -> x3, waiting for transfers between devices: none -> 25.3 us  [the longest x2 25.3 us: drive_steps_all(): side_arr = lax.ppermute(side_arr, mesh_name, queue)]
    gather x1 -> x2, local copies, waits for them, and re-layouts: 15.5 us -> 32.2 us  [matched_blocks(): return jnp.take(flat_blocks, flat_index, axis=0, mode='fill', fill_value=0)]
    ppermute x0 -> x3, starting transfers between devices: none -> 8.4 us  [the longest x2 4.97 us: drive_steps_all(): side_arr = lax.ppermute(side_arr, mesh_name, queue)]
    select_n x1 -> x2, other arithmetic: 0.02 us -> 6.34 us  [matched_blocks(): return jnp.take(flat_blocks, flat_index, axis=0, mode='fill', fill_value=0)]
    unnamed x9 -> x11, local copies, waits for them, and re-layouts: 14.4 us -> 11.4 us
    dot_general x1 -> x4, matrix products: 8.72 us -> 9.73 us  [local(): jnp.einsum('aixy,aijyz->ajxz', shard, lax.dynamic_slice_in_dim(selected,...]
  transfers between devices with their start and end apart: 5 -> 7, of which waited for: 3 -> 4; matrix products, arithmetic and copies ran while one was open for 7% -> 9% of each run, Pallas kernels for 0% -> 0%
where the time goes in v1:
time: 329 us; the launch traced here: 327 us
  waiting for transfers between devices  216 us (66%)
  local copies, waits for them, and re-layouts  54.5 us (17%)
  starting transfers between devices  29 us (9%)
  matrix products  17.4 us (5%)
  other arithmetic  9.78 us (3%)
    ppermute x4, waiting for transfers between devices, passed_along(): lax.ppermute(value, axis, [(i, (i + by) % peers) for i in range(peers)])  191 us
    gather x2, local copies, waits for them, and re-layouts, matched_blocks(): return jnp.take(flat_blocks, flat_index, axis=0, mode='fill', fill_value=0)  32.2 us
    ppermute x2, waiting for transfers between devices, drive_steps_all(): side_arr = lax.ppermute(side_arr, mesh_name, queue)  25.3 us
    ppermute x4, starting transfers between devices, passed_along(): lax.ppermute(value, axis, [(i, (i + by) % peers) for i in range(peers)])  20.6 us
    unnamed x11, local copies, waits for them, and re-layouts  11.4 us
    dot_general x4, matrix products, local(): jnp.einsum('aixy,aijyz->ajxz', shard, lax.dynamic_slice_in_dim(selected,...  9.73 us
    dot_general x1, matrix products, local(): jnp.einsum('aixy,aijyz->ajxz', values, selected, preferred_element_type=j...  7.64 us
  transfers between devices with their start and end apart: 7, of which 4 were waited for; matrix products, arithmetic and copies ran while one was open for 9% of the time, Pallas kernels for 0%

profile of v1, /device:TPU:1, one launch (start us, length us, event | category | flops | bytes accessed | tf_op | source)
XLA Modules:
  0.0 326.7 jit_solution(7080814978515853620)
XLA Ops:
  0.0 4.4 %collective-permute-start.1 = (bf16[6,16,128,128]{3,2,1,0:T(8,128)(2,1)}, bf16[6,16,128,128]{3,2,1,0:T(8,128)(2,1)}, u32[]{:S(2)}, u32[]{:S(2)}) collective-permute-start(bf16[6,16,128,128]{3,2,1,0:T(8,128)(2,1)} %param.2), channel_id=1, source_target_pairs={{0,4},{4,8},{8,12},{12,16},{16,20},{20,24},{24,28},{28,32},{32,36}... | collective-permute-start | bytes 9437192 | tf_op jit(solution)/shard_map/ppermute | solution.py:31
  4.4 7.6 %collective-permute-start.2 = (bf16[6,16,128,128]{3,2,1,0:T(8,128)(2,1)}, bf16[6,16,128,128]{3,2,1,0:T(8,128)(2,1)S(1)}, u32[]{:S(2)}, u32[]{:S(2)}) collective-permute-start(bf16[6,16,128,128]{3,2,1,0:T(8,128)(2,1)} %param.2), channel_id=1, source_target_pairs={{0,508},{4,0},{8,4},{12,8},{16,12},{20,16},{24,20},{28,24},{32,28}... | collective-permute-start | bytes 9437192 | tf_op jit(solution)/shard_map/ppermute | solution.py:31
  12.0 3.2 fusion.29
  15.2 1.9 collective-permute-start
  17.1 6.7 %collective-permute-start.3 = (bf16[2,16,128,128]{3,2,1,0:T(8,128)(2,1)}, bf16[2,16,128,128]{3,2,1,0:T(8,128)(2,1)}, u32[]{:S(2)}, u32[]{:S(2)}) collective-permute-start(bf16[2,16,128,128]{3,2,1,0:T(8,128)(2,1)} %get-tuple-element.7), channel_id=1, source_target_pairs={{0,504},{4,508},{8,0},{12,4},{16,8},{20,12},{24,16},{28,20},{32,24... | collective-permute-start | bytes 3145736 | tf_op jit(solution)/shard_map/ppermute | solution.py:31
  23.8 1.0 copy.46
  24.7 0.6 compare_and_fusion.1
  25.3 0.6 reshape.50
  25.9 0.7 pad_clamp_fusion.1
  26.6 1.4 dynamic_slice.19
  28.0 0.8 copy.48
  28.7 1.2 gather_fusion
  29.9 0.9 broadcast_select_fusion.1
  30.8 0.6 compare_reduce_fusion
  31.4 0.6 fusion.23
  32.0 0.1 copy.49
  32.1 0.1 reshape.58
  32.3 138.4 %collective-permute-done = bf16[2,16,128,128]{3,2,1,0:T(8,128)(2,1)} collective-permute-done((bf16[2,16,128,128]{3,2,1,0:T(8,128)(2,1)}, bf16[2,16,128,128]{3,2,1,0:T(8,128)(2,1)}, u32[]{:S(2)}, u32[]{:S(2)}) %collective-permute-start) | collective-permute-done | bytes 1048608 | tf_op jit(solution)/shard_map/ppermute | solution.py:31
  170.7 2.4 constant_dynamic-update-slice_fusion.4
  173.1 0.0 copy-start.2
  173.1 0.0 collective-permute-done.1
  173.1 4.1 %constant_dynamic-update-slice_fusion.3 = bf16[22,16,128,128]{3,2,1,0:T(8,128)(2,1)} fusion(bf16[22,16,128,128]{3,2,1,0:T(8,128)(2,1)} %constant_dynamic-update-slice_fusion.4, bf16[6,16,128,128]{3,2,1,0:T(8,128)(2,1)} %collective-permute-done.1), kind=kLoop, calls=%fused_computation.41 | loop fusion | bytes 6291456
  177.1 0.0 copy-done.2
  177.2 2.1 constant_dynamic-update-slice_fusion.2
  179.2 0.0 collective-permute-done.2
  179.2 1.9 constant_dynamic-update-slice_fusion.1
  181.1 52.1 %collective-permute-done.3 = bf16[2,16,128,128]{3,2,1,0:T(8,128)(2,1)} collective-permute-done((bf16[2,16,128,128]{3,2,1,0:T(8,128)(2,1)}, bf16[2,16,128,128]{3,2,1,0:T(8,128)(2,1)}, u32[]{:S(2)}, u32[]{:S(2)}) %collective-permute-start.3) | collective-permute-done | bytes 1048608 | tf_op jit(solution)/shard_map/ppermute | solution.py:31
  233.3 2.3 constant_dynamic-update-slice_fusion
  235.6 15.5 %gather_fusion.1 = bf16[384,128,128]{2,1,0:T(8,128)(2,1)} fusion(bf16[352,128,128]{2,1,0:T(8,128)(2,1)} %bitcast.1, s32[1024]{0:T(1024)S(1)} %pad_clamp_fusion), kind=kCustom, calls=%fused_computation.1 | custom fusion | bytes 25167360 | tf_op jit(solution)/shard_map/jit(_take)/gather | solution.py:50
  251.1 16.7 %copy.50 = bf16[6,16,4,128,128]{3,4,1,2,0:T(8,128)(2,1)} copy(bf16[6,16,4,128,128]{4,3,2,1,0:T(8,128)(2,1)} %bitcast.91) | data formatting | bytes 25165824 | tf_op jit(solution)/shard_map/jit(_take)/gather | solution.py:50
  267.9 6.3 %broadcast_select_fusion = bf16[6,16,4,128,128]{3,4,1,2,0:T(8,128)(2,1)S(1)} fusion(bf16[6,16,4,128,128]{3,4,1,2,0:T(8,128)(2,1)} %copy.50, pred[6,16,4]{1,2,0:T(4,128)(4,1)S(1)} %compare_and_fusion), kind=kLoop, calls=%fused_computation.2 | loop fusion | flops 6291456 | bytes 25166208 | tf_op jit(solution)/shard_map/jit(_take)/select_n | solution.py:50
  274.2 0.0 copy-start
  274.2 7.6 %fusion = f32[6,4,128,128,1]{3,2,4,1,0:T(8,128)S(1)} fusion(bf16[6,16,4,128,128]{3,4,1,2,0:T(8,128)(2,1)S(1)} %broadcast_select_fusion, bf16[6,16,128,128]{3,2,1,0:T(8,128)(2,1)} %param.2), kind=kOutput, calls=%fused_computation.3 | convolution fusion | flops 1610612736 | bytes 17301504 | tf_op jit(solution)/shard_map/aixy,aijyz->ajxz/dot_general | solution.py:76
  281.8 0.0 copy-done
  281.9 0.1 fusion.22
  282.0 3.1 collective-permute-start.5
  285.1 3.4 %collective-permute-start.4 = (bf16[6,4,128,128]{2,3,1,0:T(8,128)(2,1)S(1)}, bf16[6,4,128,128]{2,3,1,0:T(8,128)(2,1)}, u32[]{:S(2)}, u32[]{:S(2)}) collective-permute-start(bf16[6,4,128,128]{2,3,1,0:T(8,128)(2,1)S(1)} %fusion.22), channel_id=1, source_target_pairs={{0,3},{1,0},{2,1},{3,2},{4,7},{5,4},{6,5},{7,6},{8,11},{9,8},{10,9... | collective-permute-start | bytes 2359304 | tf_op jit(solution)/shard_map/ppermute | solution.py:21
  288.6 15.2 %collective-permute-done.5 = bf16[6,4,128,128]{2,3,1,0:T(8,128)(2,1)S(1)} collective-permute-done((bf16[6,4,128,128]{2,3,1,0:T(8,128)(2,1)S(1)}, bf16[6,4,128,128]{2,3,1,0:T(8,128)(2,1)S(1)}, u32[]{:S(2)}, u32[]{:S(2)}) %collective-permute-start.5) | collective-permute-done | bytes 786464 | tf_op jit(solution)/shard_map/ppermute | solution.py:19
  303.7 1.9 collective-permute-start.6
  305.6 0.0 copy-start.1
  305.6 3.0 fusion.8
  308.7 3.5 %fusion.4 = f32[6,4,128,128,1]{3,2,4,1,0:T(8,128)S(1)} fusion(bf16[6,16,4,128,128]{3,4,1,2,0:T(8,128)(2,1)} %copy-done, s32[]{:T(128)S(6)} %select_n.109, bf16[6,4,128,128]{2,3,1,0:T(8,128)(2,1)S(1)} %collective-permute-done.5), kind=kOutput, calls=%fused_computation.7 | convolution fusion | flops 402653184 | bytes 5505028 | tf_op jit(solution)/shard_map/aixy,aijyz->ajxz/dot_general | solution.py:81
  312.2 0.0 collective-permute-done.4
  312.2 0.0 copy-done.1
  312.2 2.1 fusion.6
  314.3 10.2 %collective-permute-done.6 = bf16[6,4,128,128]{2,3,1,0:T(8,128)(2,1)S(1)} collective-permute-done((bf16[6,4,128,128]{2,3,1,0:T(8,128)(2,1)S(1)}, bf16[6,4,128,128]{2,3,1,0:T(8,128)(2,1)S(1)}, u32[]{:S(2)}, u32[]{:S(2)}) %collective-permute-start.6) | collective-permute-done | bytes 786464 | tf_op jit(solution)/shard_map/ppermute | solution.py:19
  324.5 1.1 fusion.15
  325.6 1.2 copy.55
  (4 shorter events, 0.1 us)
Async XLA Ops:
  0.0 173.1 %collective-permute-start.1 = (bf16[6,16,128,128]{3,2,1,0:T(8,128)(2,1)}, bf16[6,16,128,128]{3,2,1,0:T(8,128)(2,1)}, u32[]{:S(2)}, u32[]{:S(2)}) collective-permute-start(bf16[6,16,128,128]{3,2,1,0:T(8,128)(2,1)} %param.2), channel_id=1, source_target_pairs={{0,4},{4,8},{8,12},{12,16},{16,20},{20,24},{24,28},{28,32},{32,36}... | collective-permute-start | bytes 9437192 | tf_op jit(solution)/shard_map/ppermute | solution.py:31
  4.4 174.8 %collective-permute-start.2 = (bf16[6,16,128,128]{3,2,1,0:T(8,128)(2,1)}, bf16[6,16,128,128]{3,2,1,0:T(8,128)(2,1)S(1)}, u32[]{:S(2)}, u32[]{:S(2)}) collective-permute-start(bf16[6,16,128,128]{3,2,1,0:T(8,128)(2,1)} %param.2), channel_id=1, source_target_pairs={{0,508},{4,0},{8,4},{12,8},{16,12},{20,16},{24,20},{28,24},{32,28}... | collective-permute-start | bytes 9437192 | tf_op jit(solution)/shard_map/ppermute | solution.py:31
  15.2 155.5 %collective-permute-start = (bf16[2,16,128,128]{3,2,1,0:T(8,128)(2,1)}, bf16[2,16,128,128]{3,2,1,0:T(8,128)(2,1)}, u32[]{:S(2)}, u32[]{:S(2)}) collective-permute-start(bf16[2,16,128,128]{3,2,1,0:T(8,128)(2,1)} %get-tuple-element.8), channel_id=1, source_target_pairs={{0,8},{4,12},{8,16},{12,20},{16,24},{20,28},{24,32},{28,36},{32,40... | collective-permute-start | bytes 3145736 | tf_op jit(solution)/shard_map/ppermute | solution.py:31
  17.1 216.2 %collective-permute-start.3 = (bf16[2,16,128,128]{3,2,1,0:T(8,128)(2,1)}, bf16[2,16,128,128]{3,2,1,0:T(8,128)(2,1)}, u32[]{:S(2)}, u32[]{:S(2)}) collective-permute-start(bf16[2,16,128,128]{3,2,1,0:T(8,128)(2,1)} %get-tuple-element.7), channel_id=1, source_target_pairs={{0,504},{4,508},{8,0},{12,4},{16,8},{20,12},{24,16},{28,20},{32,24... | collective-permute-start | bytes 3145736 | tf_op jit(solution)/shard_map/ppermute | solution.py:31
  173.1 4.1 %copy-start.2 = (bf16[6,16,128,128]{3,2,1,0:T(8,128)(2,1)S(1)}, bf16[6,16,128,128]{3,2,1,0:T(8,128)(2,1)}, u32[]{:S(2)}) copy-start(bf16[6,16,128,128]{3,2,1,0:T(8,128)(2,1)} %param.2) | copy-start | bytes 9437188
  274.2 7.7 %copy-start = (bf16[6,16,4,128,128]{3,4,1,2,0:T(8,128)(2,1)}, bf16[6,16,4,128,128]{3,4,1,2,0:T(8,128)(2,1)S(1)}, u32[]{:S(2)}) copy-start(bf16[6,16,4,128,128]{3,4,1,2,0:T(8,128)(2,1)S(1)} %broadcast_select_fusion) | copy-start | bytes 37748740
  282.0 21.7 %collective-permute-start.5 = (bf16[6,4,128,128]{2,3,1,0:T(8,128)(2,1)S(1)}, bf16[6,4,128,128]{2,3,1,0:T(8,128)(2,1)S(1)}, u32[]{:S(2)}, u32[]{:S(2)}) collective-permute-start(bf16[6,4,128,128]{2,3,1,0:T(8,128)(2,1)S(1)} %fusion.22), channel_id=1, source_target_pairs={{0,1},{1,2},{2,3},{3,0},{4,5},{5,6},{6,7},{7,4},{8,9},{9,10},{10,1... | collective-permute-start | bytes 2359304 | tf_op jit(solution)/shard_map/ppermute | solution.py:19
  285.1 27.2 %collective-permute-start.4 = (bf16[6,4,128,128]{2,3,1,0:T(8,128)(2,1)S(1)}, bf16[6,4,128,128]{2,3,1,0:T(8,128)(2,1)}, u32[]{:S(2)}, u32[]{:S(2)}) collective-permute-start(bf16[6,4,128,128]{2,3,1,0:T(8,128)(2,1)S(1)} %fusion.22), channel_id=1, source_target_pairs={{0,3},{1,0},{2,1},{3,2},{4,7},{5,4},{6,5},{7,6},{8,11},{9,8},{10,9... | collective-permute-start | bytes 2359304 | tf_op jit(solution)/shard_map/ppermute | solution.py:21
  303.7 20.8 %collective-permute-start.6 = (bf16[6,4,128,128]{2,3,1,0:T(8,128)(2,1)S(1)}, bf16[6,4,128,128]{2,3,1,0:T(8,128)(2,1)S(1)}, u32[]{:S(2)}, u32[]{:S(2)}) collective-permute-start(bf16[6,4,128,128]{2,3,1,0:T(8,128)(2,1)S(1)} %collective-permute-done.5), channel_id=1, source_target_pairs={{0,1},{1,2},{2,3},{3,0},{4,5},{5,6},{6,7},{7,4},{8,9},{9,10},{10,1... | collective-permute-start | bytes 2359304 | tf_op jit(solution)/shard_map/ppermute | solution.py:19
  305.6 6.6 %copy-start.1 = (bf16[6,16,4,128,128]{3,4,1,2,0:T(8,128)(2,1)S(1)}, bf16[6,16,4,128,128]{3,4,1,2,0:T(8,128)(2,1)}, u32[]{:S(2)}) copy-start(bf16[6,16,4,128,128]{3,4,1,2,0:T(8,128)(2,1)} %copy-done) | copy-start | bytes 37748740
